TPU v7x, 32 devices: a whole 2x2x4 slice. The times are simulated.
32 devices in a mesh: frame: 4 (over z), space: 8 (over y, x, core).
Axes of the slice: x: 2, y: 2, z: 4, core: 2. Of those that a mesh axis runs over, the one named last changes fastest.
Arguments:
- latents: bfloat16 [2, 4, 512, 3072], P(None, 'frame', 'space'), may hold values from -6 to 6
- target: bfloat16 [2, 4, 512, 3072], P(None, 'frame', 'space'), may hold values from -6 to 6
- timesteps: int32 [2], replicated, may hold values from 0 to 999
- valid: int32 [2, 2], replicated, may hold values from 1 to 16, as said below
- tile_mask: int32 [2, 16, 16], replicated, may hold values from 0 to 1, as said below
- w_mod: bfloat16 [256, 18432], replicated, may hold values from -0.5 to 0.5
- w_sqkv: bfloat16 [3, 3072, 2048], P(None, None, 'space'), may hold values from -0.109375 to 0.109375
- w_sout: bfloat16 [2048, 3072], P('space'), may hold values from -0.125 to 0.125
- w_tqkv: bfloat16 [3, 3072, 2048], P(None, None, 'frame'), may hold values from -0.109375 to 0.109375
- w_tout: bfloat16 [2048, 3072], P('frame'), may hold values from -0.125 to 0.125
Outputs:
- mixed: bfloat16 [2, 4, 512, 3072], P(None, 'frame', 'space')
- loss: float32 [], replicated
Inputs may be any that keep to these rules, and one draw needn't show every extreme that they name: Each video's valid frame count is 1 to 4 and valid tile count 1 to 16; video 0 is whole. `tile_mask`: entries are 0 or 1, with ones on the diagonal of every video's mask.
All inputs are finite; a program needn't handle non-finite values.
Results may differ from a plain program's by a relative error of at most 0.017.
Values may be sent and summed in bfloat16 or wider, within the bound.
A program may use at most 128 MiB of HBM per device.

v0:
```python
import math
import jax
import jax.numpy as jnp
from jax import lax
from jax.sharding import PartitionSpec as P

HEAD_DIM = 128
FREQ = 256
TILE = 32


def layer_norm(values):
    mean = jnp.mean(values, -1, keepdims=True)
    centred = values - mean
    var = jnp.mean(centred * centred, -1, keepdims=True)
    return centred * lax.rsqrt(var + 1e-06)


def time_embed(timesteps):
    half = FREQ // 2
    freqs = jnp.exp(-math.log(10000.0) * jnp.arange(half, dtype=jnp.float32) / half)
    angles = timesteps.astype(jnp.float32)[:, None] * freqs[None, :]
    return jnp.concatenate([jnp.cos(angles), jnp.sin(angles)], -1).astype(jnp.bfloat16)


def modulate(values, shift, scale):
    return (
        layer_norm(values.astype(jnp.float32)) * (1.0 + scale[:, None, None, :])
        + shift[:, None, None, :]
    ).astype(jnp.bfloat16)


def frame_attention(qkv, count, tiles, heads):
    length = qkv.shape[0]
    cols = heads * HEAD_DIM
    scale = 1.0 / math.sqrt(HEAD_DIM)
    query = jnp.transpose(qkv[:, :cols].reshape(length, heads, HEAD_DIM), (1, 0, 2))
    keys = jnp.transpose(qkv[:, cols : 2 * cols].reshape(length, heads, HEAD_DIM), (1, 0, 2))
    values = jnp.transpose(qkv[:, 2 * cols :].reshape(length, heads, HEAD_DIM), (1, 0, 2))
    tile_ids = jnp.arange(length, dtype=jnp.int32) // TILE
    expanded = jnp.repeat(jnp.repeat(tiles, TILE, axis=0), TILE, axis=1)
    allowed = (expanded == 1) & (tile_ids[None, :] < count) | (
        tile_ids[:, None] == tile_ids[None, :]
    )

    def one_head(parts):
        q_head, k_head, v_head = parts
        scores = (
            lax.dot_general(
                q_head, k_head, (((1,), (1,)), ((), ())), preferred_element_type=jnp.float32
            )
            * scale
        )
        scores = jnp.where(allowed, scores, -1e30)
        top = jnp.max(scores, -1, keepdims=True)
        weights = jnp.exp(scores - top)
        probs = (weights / jnp.sum(weights, -1, keepdims=True)).astype(jnp.bfloat16)
        return jnp.dot(probs, v_head, preferred_element_type=jnp.float32).astype(jnp.bfloat16)

    outs = lax.map(one_head, (query, keys, values))
    return jnp.transpose(outs, (1, 0, 2)).reshape(length, cols)


def temporal_attention(qkv, count, heads):
    frames, places = (qkv.shape[0], qkv.shape[1])
    cols = heads * HEAD_DIM
    scale = 1.0 / math.sqrt(HEAD_DIM)
    query = qkv[..., :cols].reshape(frames, places, heads, HEAD_DIM)
    keys = qkv[..., cols : 2 * cols].reshape(frames, places, heads, HEAD_DIM)
    values = qkv[..., 2 * cols :].reshape(frames, places, heads, HEAD_DIM)
    scores = jnp.einsum("fphd,gphd->phfg", query, keys, preferred_element_type=jnp.float32) * scale
    frame_ids = jnp.arange(frames, dtype=jnp.int32)
    allowed = (frame_ids[None, :] < count) | (frame_ids[:, None] == frame_ids[None, :])
    scores = jnp.where(allowed, scores, -1e30)
    top = jnp.max(scores, -1, keepdims=True)
    weights = jnp.exp(scores - top)
    probs = (weights / jnp.sum(weights, -1, keepdims=True)).astype(jnp.bfloat16)
    outs = jnp.einsum("phfg,gphd->fphd", probs, values, preferred_element_type=jnp.float32).astype(
        jnp.bfloat16
    )
    return outs.reshape(frames, places, cols)


def group_project(attended, w_out, groups):
    rows = attended.shape[0]
    width = w_out.shape[1]
    parts = attended.reshape(rows, groups, -1)
    weights = w_out.reshape(groups, -1, width)
    terms = jnp.einsum("rgc,gcd->rgd", parts, weights, preferred_element_type=jnp.float32).astype(
        jnp.bfloat16
    )
    return jnp.sum(terms.astype(jnp.float32), axis=1)


def shards(latents, target, timesteps, valid, tile_mask, w_mod, w_sqkv, w_sout, w_tqkv, w_tout):
    videos, frames_dev, span_dev, width = latents.shape
    space_count = lax.axis_size("space")
    frame_count = lax.axis_size("frame")
    embed = time_embed(timesteps)
    mod = jnp.dot(embed, w_mod, preferred_element_type=jnp.float32)
    shift_one, scale_one, gate_one, shift_two, scale_two, gate_two = jnp.split(mod, 6, axis=1)
    h_one = modulate(latents, shift_one, scale_one)
    spatial_heads = w_sqkv.shape[2] // HEAD_DIM
    w_flat = jnp.concatenate([w_sqkv[0], w_sqkv[1], w_sqkv[2]], axis=1)
    qkv_space = jnp.dot(
        lax.all_gather(h_one, "space", axis=2, tiled=True),
        w_flat,
        preferred_element_type=jnp.float32,
    ).astype(jnp.bfloat16)
    span = qkv_space.shape[2]
    frames_flat = qkv_space.reshape(videos * frames_dev, span, -1)
    tile_counts = jnp.repeat(valid[:, 1], frames_dev)
    tiles = jnp.repeat(tile_mask, frames_dev, axis=0)

    def per_frame(parts):
        frame_qkv, count, tiles_one = parts
        return frame_attention(frame_qkv, count, tiles_one, spatial_heads)

    spatial_att = lax.map(per_frame, (frames_flat, tile_counts, tiles)).reshape(
        videos, frames_dev, span, -1
    )
    spatial_att = jnp.transpose(spatial_att, (2, 0, 1, 3))
    w_sall = lax.all_gather(w_sout, "space", axis=0, tiled=True)
    own_rows = lax.all_to_all(spatial_att, "space", split_axis=0, concat_axis=3, tiled=True)
    spatial = group_project(
        own_rows.reshape(span_dev * videos * frames_dev, -1), w_sall, space_count
    )
    spatial = spatial.reshape(span_dev, videos, frames_dev, width)
    spatial = jnp.transpose(spatial, (1, 2, 0, 3))
    x_one = (latents.astype(jnp.float32) + gate_one[:, None, None, :] * spatial).astype(
        jnp.bfloat16
    )
    h_two = modulate(x_one, shift_two, scale_two)
    temporal_heads = w_tqkv.shape[2] // HEAD_DIM
    w_tflat = jnp.concatenate([w_tqkv[0], w_tqkv[1], w_tqkv[2]], axis=1)
    qkv_frame = jnp.dot(
        lax.all_gather(h_two, "frame", axis=1, tiled=True),
        w_tflat,
        preferred_element_type=jnp.float32,
    ).astype(jnp.bfloat16)

    def per_video(parts):
        video_qkv, count = parts
        return temporal_attention(video_qkv, count, temporal_heads)

    temporal_att = lax.map(per_video, (qkv_frame, valid[:, 0]))
    temporal_att = jnp.transpose(temporal_att, (1, 0, 2, 3))
    w_tall = lax.all_gather(w_tout, "frame", axis=0, tiled=True)
    own_frames = lax.all_to_all(temporal_att, "frame", split_axis=0, concat_axis=3, tiled=True)
    temporal = group_project(
        own_frames.reshape(frames_dev * videos * span_dev, -1), w_tall, frame_count
    )
    temporal = temporal.reshape(frames_dev, videos, span_dev, width)
    temporal = jnp.transpose(temporal, (1, 0, 2, 3))
    mixed = (x_one.astype(jnp.float32) + gate_two[:, None, None, :] * temporal).astype(jnp.bfloat16)
    diff = mixed.astype(jnp.float32) - target.astype(jnp.float32)
    squares = jnp.mean(diff * diff, -1)
    frame_ids = lax.axis_index("frame") * frames_dev + jnp.arange(frames_dev, dtype=jnp.int32)
    tile_ids = (lax.axis_index("space") * span_dev + jnp.arange(span_dev, dtype=jnp.int32)) // TILE
    mask = (frame_ids[None, :, None] < valid[:, 0][:, None, None]) & (
        tile_ids[None, None, :] < valid[:, 1][:, None, None]
    )
    local_total = jnp.sum(jnp.where(mask, squares, 0.0))
    total = lax.psum(local_total, ("frame", "space"))
    count = jnp.sum(valid[:, 0] * valid[:, 1]).astype(jnp.float32) * TILE
    return (mixed, total / count)


def solution(mesh):
    return jax.shard_map(
        shards,
        mesh=mesh,
        in_specs=(
            P(None, "frame", "space", None),
            P(None, "frame", "space", None),
            P(),
            P(),
            P(),
            P(),
            P(None, None, "space"),
            P("space", None),
            P(None, None, "frame"),
            P("frame", None),
        ),
        out_specs=(P(None, "frame", "space", None), P()),
        check_vma=False,
    )
```

profile of v0, /device:TPU:12, one launch (start us, length us, event | category | flops | bytes accessed | tf_op | source)
XLA Modules:
  0.0 503.2 jit_solution(8383597021539726154)
XLA Ops:
  8.0 5.1 %fusion.68 = f32[2,18432]{1,0:T(2,128)S(1)} fusion(bf16[256,18432]{1,0:T(8,128)(2,1)} %param.21, bf16[2,128]{1,0:T(2,128)(2,1)S(1)} %get-tuple-element.260, bf16[2,128]{1,0:T(2,128)(2,1)S(1)} %get-tuple-element.259), kind=kOutput, calls=%fused_computation.113 | convolution fusion | flops 18876416 | bytes 9585664 | tf_op jit(solution)/shard_map/dot_general | solution.py:100
  16.0 4.4 slice_bitcast_fusion.5
  20.4 41.2 %all-gather.5.cloned.1.call-done = bf16[2,1,512,3072]{3,2,0,1:T(8,128)(2,1)} async-done(((bf16[2,1,64,3072]{3,2,0,1:T(8,128)(2,1)}), bf16[2,1,512,3072]{3,2,0,1:T(8,128)(2,1)}) %all-gather.5.cloned.1.call-update) | async-done | bytes 6291472 | tf_op jit(solution)/shard_map/all_gather | solution.py:106
  61.6 9.9 %fusion.52 = bf16[2,512,768]{2,1,0:T(8,128)(2,1)} fusion(bf16[3072,256]{1,0:T(8,128)(2,1)} %get-tuple-element.251, bf16[3072,256]{1,0:T(8,128)(2,1)} %get-tuple-element.252, bf16[3072,256]{1,0:T(8,128)(2,1)S(1)} %get-tuple-element.250, bf16[2,1,512,3072]{3,2,0,1:T(8,128)(2,1)} %all-gather.5.cloned.1.call-done), kind=kOutput, calls=%fused_computation.84 | convolution fusion | flops 4846780416 | bytes 12582912 | tf_op jit(solution)/shard_map/dot_general | solution.py:105
  71.4 12.7 %while.43 = (s32[]{:T(128)}, bf16[2,512,256]{2,1,0:T(8,128)(2,1)S(1)}, bf16[2,512,768]{2,1,0:T(8,128)(2,1)}, s32[2,16,16]{2,1,0:T(8,128)S(1)}, s32[2]{0:T(128)S(1)}, /*index=5*/s32[]{:T(128)}, s32[]{:T(128)}, s32[]{:T(128)}) while((s32[]{:T(128)}, bf16[2,512,256]{2,1,0:T(8,128)(2,1)S(1)}, bf16[2,512,768]{2,1,0:T(8,128)(2,1)}, ...), condition=%wide.region_7.8_spmd, body=%wide.region_2.7_spmd.sunk | while | flops 137174784 | bytes 10541854 | solution.py:119
  71.4 1.3 constant_dynamic-slice_fusion.4
  74.7 2.7 while.45
  81.0 2.7 while.45
  84.7 12.6 %all_to_all.30 = bf16[512,2,1,256]{3,1,2,0:T(2,128)(2,1)S(1)} all-to-all(bf16[512,2,1,256]{3,1,2,0:T(2,128)(2,1)S(1)} %bitcast.158), channel_id=1, replica_groups=mesh['frame'=4,'space'=8] {'space'}, dimensions={0} | all-to-all | bytes 1048576 | tf_op jit(solution)/shard_map/all_to_all | solution.py:124
  97.5 42.3 %all-gather.7.cloned.1.call-done = bf16[2048,3072]{1,0:T(8,128)(2,1)} async-done(((bf16[256,3072]{1,0:T(8,128)(2,1)}), bf16[2048,3072]{1,0:T(8,128)(2,1)}) %all-gather.7.cloned.1.call-update) | async-done | bytes 12582928 | tf_op jit(solution)/shard_map/all_gather | solution.py:123
  139.8 7.7 %convert_reduce_fusion = f32[128,3072]{1,0:T(8,128)} fusion(bf16[128,8,256]{2,0,1:T(8,128)(2,1)S(1)} %reshape_reshape.6, bf16[8,256,3072]{2,1,0:T(8,128)(2,1)} %bitcast.152), kind=kOutput, calls=%fused_computation.53 | convolution fusion | flops 1619656704 | bytes 14680064 | tf_op jit(solution)/shard_map/rgc,gcd->rgd/dot_general | solution.py:89
  147.5 2.2 reshape.315
  150.8 1.3 fusion.58
  152.7 6.7 %slice_bitcast_fusion.2 = (bf16[3072,512]{1,0:T(8,128)(2,1)}, bf16[3072,512]{1,0:T(8,128)(2,1)}, bf16[3072,512]{1,0:T(8,128)(2,1)}) fusion(bf16[3,3072,512]{2,1,0:T(8,128)(2,1)} %param.24), kind=kLoop, calls=%fused_computation.72 | loop fusion | bytes 18874368 | tf_op jit(solution)/shard_map/squeeze | solution.py:135
  159.5 54.6 %all-gather.9.cloned.1.call-done = bf16[2,4,64,3072]{3,2,0,1:T(8,128)(2,1)} async-done(((bf16[2,1,64,3072]{3,2,0,1:T(8,128)(2,1)}), bf16[2,4,64,3072]{3,2,0,1:T(8,128)(2,1)}) %all-gather.9.cloned.1.call-update) | async-done | bytes 3145744 | tf_op jit(solution)/shard_map/all_gather | solution.py:137
  214.0 9.7 %fusion.45 = bf16[2,4,64,1536]{3,2,1,0:T(8,128)(2,1)S(1)} fusion(bf16[3072,512]{1,0:T(8,128)(2,1)} %get-tuple-element.248, bf16[3072,512]{1,0:T(8,128)(2,1)} %get-tuple-element.249, bf16[3072,512]{1,0:T(8,128)(2,1)} %get-tuple-element.247, bf16[2,4,64,3072]{3,2,0,1:T(8,128)(2,1)} %all-gather.9.cloned.1.call-done), kind=kOutput, calls=%fused_computation.73 | convolution fusion | flops 4860936192 | bytes 14155776 | tf_op jit(solution)/shard_map/dot_general | solution.py:136
  223.7 11.9 %while.44 = (s32[]{:T(128)}, bf16[2,4,64,512]{3,2,0,1:T(8,128)(2,1)}, bf16[2,4,64,1536]{3,2,1,0:T(8,128)(2,1)S(1)}, s32[2]{0:T(128)S(1)}, s32[]{:T(128)}) while((s32[]{:T(128)}, bf16[2,4,64,512]{3,2,0,1:T(8,128)(2,1)}, bf16[2,4,64,1536]{3,2,1,0:T(8,128)(2,1)S(1)}, s32[2]{0:T(128)S(1)}, s32[]{:T(128)}) %tuple.106), condition=%wide.region_14.15_spmd, body=%wide.region_11.14_spmd.sunk | while | flops 2252841 | bytes 7479929 | solution.py:146
  224.7 1.4 fusion.109
  230.7 1.4 fusion.109
  235.6 6.2 %all-to-all-start.1 = ((bf16[4,2,64,512]{3,2,1,0:T(8,128)(2,1)}), bf16[4,2,64,512]{3,2,1,0:T(8,128)(2,1)S(1)}, u32[]{:S(2)}, u32[]{:S(2)}) async-start(bf16[4,2,64,512]{3,2,1,0:T(8,128)(2,1)} %bitcast.161), calls=%async_computation.1 | async-start | bytes 1048576 | tf_op jit(solution)/shard_map/all_to_all | solution.py:149
  243.1 198.7 %all-gather.11.cloned.1.call-done = bf16[2048,3072]{1,0:T(8,128)(2,1)} async-done(((bf16[512,3072]{1,0:T(8,128)(2,1)}), bf16[2048,3072]{1,0:T(8,128)(2,1)}) %all-gather.11.cloned.1.call-update) | async-done | bytes 12582928 | tf_op jit(solution)/shard_map/all_gather | solution.py:148
  441.8 6.6 %convert_reduce_fusion.1 = f32[128,3072]{1,0:T(8,128)S(1)} fusion(bf16[128,4,512]{2,0,1:T(8,128)(2,1)S(1)} %bitcast.157, bf16[4,512,3072]{2,1,0:T(8,128)(2,1)} %bitcast.153), kind=kOutput, calls=%fused_computation.62 | convolution fusion | flops 1614938112 | bytes 14680064 | tf_op jit(solution)/shard_map/rgc,gcd->rgd/dot_general | solution.py:89
  448.4 1.4 multiply_reduce_fusion
  450.5 44.4 %psum.7 = f32[]{:T(128)} all-reduce(f32[]{:T(128)} %fusion.67), channel_id=1, replica_groups=mesh['frame'=4,'space'=8] {'frame','space'}, use_global_device_ids=true, to_apply=%region_18.19 | all-reduce | flops 1 | bytes 8 | tf_op jit(solution)/shard_map/psum | solution.py:164
  (116 shorter events, 27.3 us)
Async XLA Ops:
  7.2 54.4 %all-gather.5.cloned.1.call-start = ((), (), s32[]{:S(2)}) async-start(), calls=%async_computation.2 | async-start | bytes 7077888 | tf_op jit(solution)/shard_map/all_gather | solution.py:106
  8.0 5.1 %copy-start = (bf16[2,1,64,3072]{3,2,1,0:T(8,128)(2,1)S(1)}, bf16[2,1,64,3072]{3,2,1,0:T(8,128)(2,1)}, u32[]{:S(2)}) copy-start(bf16[2,1,64,3072]{3,2,1,0:T(8,128)(2,1)} %param.16) | copy-start | bytes 2359300
  15.0 0.8 copy-start.3
  15.0 124.8 %all-gather.7.cloned.1.call-start = ((), (), s32[]{:S(2)}) async-start(), calls=%async_computation.3 | async-start | bytes 14155776 | tf_op jit(solution)/shard_map/all_gather | solution.py:123
  15.8 198.3 %all-gather.9.cloned.1.call-start = ((), (), s32[]{:S(2)}) async-start(), calls=%async_computation.4 | async-start | bytes 3932160 | tf_op jit(solution)/shard_map/all_gather | solution.py:137
  61.6 9.9 %copy-start.2 = (s32[2,16,16]{2,1,0:T(8,128)S(1)}, s32[2,16,16]{2,1,0:T(8,128)}, u32[]{:S(2)}) copy-start(s32[2,16,16]{2,1,0:T(8,128)} %param.20) | copy-start | bytes 6148
  152.1 289.7 %all-gather.11.cloned.1.call-start = ((), (), s32[]{:S(2)}) async-start(), calls=%async_computation.5 | async-start | bytes 15728640 | tf_op jit(solution)/shard_map/all_gather | solution.py:148
  235.6 206.2 %all-to-all-start.1 = ((bf16[4,2,64,512]{3,2,1,0:T(8,128)(2,1)}), bf16[4,2,64,512]{3,2,1,0:T(8,128)(2,1)S(1)}, u32[]{:S(2)}, u32[]{:S(2)}) async-start(bf16[4,2,64,512]{3,2,1,0:T(8,128)(2,1)} %bitcast.161), calls=%async_computation.1 | async-start | bytes 1048576 | tf_op jit(solution)/shard_map/all_to_all | solution.py:149
  441.8 6.6 %copy-start.1 = (bf16[2,1,64,3072]{3,2,1,0:T(8,128)(2,1)S(1)}, bf16[2,1,64,3072]{3,2,1,0:T(8,128)(2,1)}, u32[]{:S(2)}) copy-start(bf16[2,1,64,3072]{3,2,1,0:T(8,128)(2,1)} %param.17) | copy-start | bytes 2359300
Sparse Core Ops, SparseCore 0:
  15.1 46.3 all-gather.4
  63.5 76.3 all-gather.6
  152.2 61.7 all-gather.8
  215.5 226.2 all-gather.10
where the time goes:
time: 504 us; the launch traced here: 503 us
  waiting for transfers between devices  338 us (67%)
  blocking collectives  57 us (11%)
  matrix products  45.9 us (9%)
  local copies, waits for them, and re-layouts  26.5 us (5%)
  between operations  16.3 us (3%)
  other arithmetic  12.6 us (2%)
  starting transfers between devices  6.4 us (1%)
    all_gather x1, waiting for transfers between devices, shards(): w_tall = lax.all_gather(w_tout, 'frame', axis=0, tiled=True)  199 us
    all_gather x1, waiting for transfers between devices, shards(): lax.all_gather(h_two, 'frame', axis=1, tiled=True)  54.6 us
    psum x1, blocking collectives, shards(): total = lax.psum(local_total, ('frame', 'space'))  44.4 us
    all_gather x1, waiting for transfers between devices, shards(): w_sall = lax.all_gather(w_sout, 'space', axis=0, tiled=True)  42.3 us
    all_gather x1, waiting for transfers between devices, shards(): lax.all_gather(h_one, 'space', axis=2, tiled=True)  41.2 us
    dot_general x2, matrix products, group_project(): jnp.einsum('rgc,gcd->rgd', parts, weights, preferred_element_type=jnp.flo...  14.3 us
    all_to_all x1, blocking collectives, shards(): lax.all_to_all(spatial_att, 'space', split_axis=0, concat_axis=3, tiled=T...  12.6 us
  transfers between devices with their start and end apart: 5, of which 4 were waited for; matrix products, arithmetic and copies ran while one was open for 11% of the time, Pallas kernels for 0%

commit v1 on v0

--- a/solution.py
+++ b/solution.py
@@ -7,6 +7,28 @@
 HEAD_DIM = 128
 FREQ = 256
 TILE = 32
+
+
+def joined_along(tiles, dim):
+    dims = list(tiles.shape[1:])
+    dims[dim] *= tiles.shape[0]
+    return jnp.moveaxis(tiles, 0, dim).reshape(dims)
+
+
+def ring_gather(x, axis, dim):
+    peers = lax.axis_size(axis)
+    pairs = [(i, (i + 1) % peers) for i in range(peers)]
+    back = [(b, a) for a, b in pairs]
+    lower, upper = ([], [])
+    for step in range(peers - 1):
+        if step % 2 == 0:
+            lower.append(lax.ppermute(lower[-1] if lower else x, axis, pairs))
+        else:
+            upper.append(lax.ppermute(upper[-1] if upper else x, axis, back))
+    blocks = jnp.stack([*lower[::-1], x, *upper])
+    shift = lax.axis_index(axis) - len(lower)
+    blocks = blocks[(jnp.arange(peers) - shift) % peers]
+    return joined_along(blocks, dim)
 
 
 def layer_norm(values):
@@ -145,7 +167,7 @@
 
     temporal_att = lax.map(per_video, (qkv_frame, valid[:, 0]))
     temporal_att = jnp.transpose(temporal_att, (1, 0, 2, 3))
-    w_tall = lax.all_gather(w_tout, "frame", axis=0, tiled=True)
+    w_tall = ring_gather(w_tout, "frame", 0)
     own_frames = lax.all_to_all(temporal_att, "frame", split_axis=0, concat_axis=3, tiled=True)
     temporal = group_project(
         own_frames.reshape(frames_dev * videos * span_dev, -1), w_tall, frame_count

time: 504 us -> 487 us (0.966)
  waiting for transfers between devices: 338 us -> 267 us
  local copies, waits for them, and re-layouts: 26.5 us -> 69.6 us
  blocking collectives: 57 us -> 41.5 us
  starting transfers between devices: 6.4 us -> 20.1 us
  other arithmetic: 12.6 us -> 24.1 us
    all_gather x1 -> x0, waiting for transfers between devices: 199 us -> none  [shards(): w_tall = lax.all_gather(w_tout, 'frame', axis=0, tiled=True)]
    ppermute x0 -> x3, waiting for transfers between devices: none -> 181 us  [the longest x1 115 us: ring_gather(): upper.append(lax.ppermute(upper[-1] if upper else x, axis, back))]
    all_gather x1, waiting for transfers between devices: 54.6 us -> 0.01 us  [shards(): lax.all_gather(h_two, 'frame', axis=1, tiled=True)]
    gather x0 -> x5, local copies, waits for them, and re-layouts: none -> 40.3 us  [ring_gather(): blocks = blocks[(jnp.arange(peers) - shift) % peers]]
    all_to_all x1 -> x0, blocking collectives: 12.6 us -> none  [shards(): lax.all_to_all(spatial_att, 'space', split_axis=0, concat_axis=3, tiled=T...]
    ppermute x0 -> x3, starting transfers between devices: none -> 9.96 us  [the longest x2 9.37 us: ring_gather(): lower.append(lax.ppermute(lower[-1] if lower else x, axis, pairs))]
    another operation x3 -> x4, other arithmetic: 0.11 us -> 9.65 us  [the longest x1 9.53 us: ring_gather(): blocks = jnp.stack([*lower[::-1], x, *upper])]
    all_to_all x0 -> x1, waiting for transfers between devices: none -> 6.79 us  [shards(): lax.all_to_all(spatial_att, 'space', split_axis=0, concat_axis=3, tiled=T...]
  transfers between devices with their start and end apart: 5 -> 8, of which waited for: 4 -> 6; matrix products, arithmetic and copies ran while one was open for 11% -> 20% of each run, Pallas kernels for 0% -> 0%
where the time goes in v1:
time: 487 us; the launch traced here: 485 us
  waiting for transfers between devices  267 us (55%)
  local copies, waits for them, and re-layouts  69.6 us (14%)
  matrix products  45.8 us (9%)
  blocking collectives  41.5 us (9%)
  other arithmetic  24.1 us (5%)
  starting transfers between devices  20.1 us (4%)
  between operations  16.3 us (3%)
    ppermute x1, waiting for transfers between devices, ring_gather(): upper.append(lax.ppermute(upper[-1] if upper else x, axis, back))  115 us
    ppermute x2, waiting for transfers between devices, ring_gather(): lower.append(lax.ppermute(lower[-1] if lower else x, axis, pairs))  66.5 us
    psum x1, blocking collectives, shards(): total = lax.psum(local_total, ('frame', 'space'))  41.5 us
    all_gather x1, waiting for transfers between devices, shards(): lax.all_gather(h_one, 'space', axis=2, tiled=True)  41.2 us
    gather x5, local copies, waits for them, and re-layouts, ring_gather(): blocks = blocks[(jnp.arange(peers) - shift) % peers]  40.3 us
    all_gather x1, waiting for transfers between devices, shards(): w_sall = lax.all_gather(w_sout, 'space', axis=0, tiled=True)  37.2 us
    dot_general x2, matrix products, group_project(): jnp.einsum('rgc,gcd->rgd', parts, weights, preferred_element_type=jnp.flo...  14.2 us
    dot_general x1, matrix products, shards(): jnp.dot(lax.all_gather(h_one, 'space', axis=2, tiled=True), w_flat, prefe...  9.87 us
  transfers between devices with their start and end apart: 8, of which 6 were waited for; matrix products, arithmetic and copies ran while one was open for 20% of the time, Pallas kernels for 0%

profile of v1, /device:TPU:12, one launch (start us, length us, event | category | flops | bytes accessed | tf_op | source)
XLA Modules:
  0.0 484.8 jit_solution(7611240742492585446)
XLA Ops:
  8.0 5.1 %fusion.77 = f32[2,18432]{1,0:T(2,128)S(1)} fusion(bf16[256,18432]{1,0:T(8,128)(2,1)} %param.21, bf16[2,128]{1,0:T(2,128)(2,1)S(1)} %get-tuple-element.262, bf16[2,128]{1,0:T(2,128)(2,1)S(1)} %get-tuple-element.261), kind=kOutput, calls=%fused_computation.125 | convolution fusion | flops 18876416 | bytes 9585664 | tf_op jit(solution)/shard_map/dot_general | solution.py:122
  16.5 4.4 slice_bitcast_fusion.5
  20.9 41.2 %all-gather.4.cloned.1.call-done = bf16[2,1,512,3072]{3,2,0,1:T(8,128)(2,1)} async-done(((bf16[2,1,64,3072]{3,2,0,1:T(8,128)(2,1)}), bf16[2,1,512,3072]{3,2,0,1:T(8,128)(2,1)}) %all-gather.4.cloned.1.call-update) | async-done | bytes 6291472 | tf_op jit(solution)/shard_map/all_gather | solution.py:128
  62.2 9.9 %fusion.59 = bf16[2,512,768]{2,1,0:T(8,128)(2,1)} fusion(bf16[3072,256]{1,0:T(8,128)(2,1)} %get-tuple-element.253, bf16[3072,256]{1,0:T(8,128)(2,1)} %get-tuple-element.254, bf16[3072,256]{1,0:T(8,128)(2,1)S(1)} %get-tuple-element.252, bf16[2,1,512,3072]{3,2,0,1:T(8,128)(2,1)} %all-gather.4.cloned.1.call-done), kind=kOutput, calls=%fused_computation.91 | convolution fusion | flops 4846780416 | bytes 12582912 | tf_op jit(solution)/shard_map/dot_general | solution.py:127
  72.0 12.7 %while.43 = (s32[]{:T(128)}, bf16[2,512,256]{2,1,0:T(8,128)(2,1)S(1)}, bf16[2,512,768]{2,1,0:T(8,128)(2,1)}, s32[2,16,16]{2,1,0:T(8,128)S(1)}, s32[2]{0:T(128)S(1)}, /*index=5*/s32[]{:T(128)}, s32[]{:T(128)}, s32[]{:T(128)}) while((s32[]{:T(128)}, bf16[2,512,256]{2,1,0:T(8,128)(2,1)S(1)}, bf16[2,512,768]{2,1,0:T(8,128)(2,1)}, ...), condition=%wide.region_7.8_spmd, body=%wide.region_2.7_spmd.sunk | while | flops 137174784 | bytes 10541854 | solution.py:141
  91.8 6.8 %all-to-all-done = bf16[512,2,1,256]{3,1,2,0:T(2,128)(2,1)S(1)} async-done(((bf16[512,2,1,256]{3,1,2,0:T(2,128)(2,1)}), bf16[512,2,1,256]{3,1,2,0:T(2,128)(2,1)S(1)}, u32[]{:S(2)}, u32[]{:S(2)}) %all-to-all-start) | async-done | bytes 524320 | tf_op jit(solution)/shard_map/all_to_all | solution.py:146
  98.8 37.2 %all-gather.6.cloned.1.call-done = bf16[2048,3072]{1,0:T(8,128)(2,1)} async-done(((bf16[256,3072]{1,0:T(8,128)(2,1)}), bf16[2048,3072]{1,0:T(8,128)(2,1)}) %all-gather.6.cloned.1.call-update) | async-done | bytes 12582928 | tf_op jit(solution)/shard_map/all_gather | solution.py:145
  136.0 6.5 %convert_reduce_fusion = f32[128,3072]{1,0:T(8,128)S(1)} fusion(bf16[128,8,256]{2,0,1:T(8,128)(2,1)S(1)} %reshape_reshape.6, bf16[8,256,3072]{2,1,0:T(8,128)(2,1)} %bitcast.157), kind=kOutput, calls=%fused_computation.60 | convolution fusion | flops 1619656704 | bytes 14680064 | tf_op jit(solution)/shard_map/rgc,gcd->rgd/dot_general | solution.py:111
  148.9 17.0 %collective-permute-done = bf16[512,3072]{1,0:T(8,128)(2,1)} collective-permute-done((bf16[512,3072]{1,0:T(8,128)(2,1)}, bf16[512,3072]{1,0:T(8,128)(2,1)}, u32[]{:S(2)}, u32[]{:S(2)}) %collective-permute-start) | collective-permute-done | bytes 3145760 | tf_op jit(solution)/shard_map/ppermute | solution.py:25
  165.9 7.9 %collective-permute-start.1 = (bf16[512,3072]{1,0:T(8,128)(2,1)}, bf16[512,3072]{1,0:T(8,128)(2,1)}, u32[]{:S(2)}, u32[]{:S(2)}) collective-permute-start(bf16[512,3072]{1,0:T(8,128)(2,1)} %collective-permute-done), channel_id=1, source_target_pairs={{0,8},{8,16},{16,24},{24,0},{1,9},{9,17},{17,25},{25,1},{2,10},{10... | collective-permute-start | bytes 9437192 | tf_op jit(solution)/shard_map/ppermute | solution.py:25
  175.1 7.0 %slice_bitcast_fusion.2 = (bf16[3072,512]{1,0:T(8,128)(2,1)}, bf16[3072,512]{1,0:T(8,128)(2,1)}, bf16[3072,512]{1,0:T(8,128)(2,1)}) fusion(bf16[3,3072,512]{2,1,0:T(8,128)(2,1)} %param.24), kind=kLoop, calls=%fused_computation.79 | loop fusion | bytes 18874368 | tf_op jit(solution)/shard_map/squeeze | solution.py:157
  182.1 114.6 %collective-permute-done.2 = bf16[512,3072]{1,0:T(8,128)(2,1)} collective-permute-done((bf16[512,3072]{1,0:T(8,128)(2,1)}, bf16[512,3072]{1,0:T(8,128)(2,1)}, u32[]{:S(2)}, u32[]{:S(2)}) %collective-permute-start.2) | collective-permute-done | bytes 3145760 | tf_op jit(solution)/shard_map/ppermute | solution.py:27
  296.7 49.5 %collective-permute-done.1 = bf16[512,3072]{1,0:T(8,128)(2,1)} collective-permute-done((bf16[512,3072]{1,0:T(8,128)(2,1)}, bf16[512,3072]{1,0:T(8,128)(2,1)}, u32[]{:S(2)}, u32[]{:S(2)}) %collective-permute-start.1) | collective-permute-done | bytes 3145760 | tf_op jit(solution)/shard_map/ppermute | solution.py:25
  346.1 9.5 %pad_maximum_fusion = bf16[4,512,3072]{2,1,0:T(8,128)(2,1)} fusion(bf16[1,512,3072]{2,1,0:T(8,128)(2,1)} %bitcast.28, bf16[1,512,3072]{2,1,0:T(8,128)(2,1)S(1)} %bitcast.161, bf16[1,512,3072]{2,1,0:T(8,128)(2,1)} %bitcast.26, bf16[1,512,3072]{2,1,0:T(8,128)(2,1)} %bitcast.25), kind=kLoop, calls=%fused_computation.55 | loop fusion | flops 18874368 | bytes 25165824 | tf_op jit(solution)/shard_map/stack | solution.py:28
  355.7 9.7 %fusion.52 = bf16[2,4,64,1536]{3,2,1,0:T(8,128)(2,1)S(1)} fusion(bf16[3072,512]{1,0:T(8,128)(2,1)} %get-tuple-element.250, bf16[3072,512]{1,0:T(8,128)(2,1)} %get-tuple-element.251, bf16[3072,512]{1,0:T(8,128)(2,1)} %get-tuple-element.249, bf16[2,4,64,3072]{3,2,0,1:T(8,128)(2,1)} %all-gather.8.cloned.1.call-done), kind=kOutput, calls=%fused_computation.80 | convolution fusion | flops 4860936192 | bytes 14155776 | tf_op jit(solution)/shard_map/dot_general | solution.py:158
  365.4 11.8 %while.44 = (s32[]{:T(128)}, bf16[2,4,64,512]{3,2,0,1:T(8,128)(2,1)}, bf16[2,4,64,1536]{3,2,1,0:T(8,128)(2,1)S(1)}, s32[2]{0:T(128)S(1)}, s32[]{:T(128)}) while((s32[]{:T(128)}, bf16[2,4,64,512]{3,2,0,1:T(8,128)(2,1)}, bf16[2,4,64,1536]{3,2,1,0:T(8,128)(2,1)S(1)}, s32[2]{0:T(128)S(1)}, s32[]{:T(128)}) %tuple.107), condition=%wide.region_14.15_spmd, body=%wide.region_11.14_spmd.sunk | while | flops 2252841 | bytes 7479929 | solution.py:168
  377.1 5.8 %all-to-all-start.1 = ((bf16[4,2,64,512]{3,2,1,0:T(8,128)(2,1)}), bf16[4,2,64,512]{3,2,1,0:T(8,128)(2,1)S(1)}, u32[]{:S(2)}, u32[]{:S(2)}) async-start(bf16[4,2,64,512]{3,2,1,0:T(8,128)(2,1)} %bitcast.165), calls=%async_computation.1 | async-start | bytes 1048576 | tf_op jit(solution)/shard_map/all_to_all | solution.py:171
  383.0 10.3 %fusion.93 = (bf16[4,512,1536]{2,1,0:T(8,128)(2,1)}, bf16[4,512,1536]{2,1,0:T(8,128)(2,1)}) fusion(bf16[4,512,3072]{2,1,0:T(8,128)(2,1)} %pad_maximum_fusion), kind=kLoop, calls=%fused_computation.148 | loop fusion | bytes 25165824 | tf_op jit(solution)/shard_map/gather | solution.py:30
  393.2 6.4 %gather_fusion = bf16[4,512,1536]{2,1,0:T(8,128)(2,1)} fusion(bf16[4,512,1536]{2,1,0:T(8,128)(2,1)} %get-tuple-element.247, s32[1024]{0:T(1024)S(1)} %pad_clamp_fusion), kind=kCustom, calls=%fused_computation | custom fusion | bytes 12582928 | tf_op jit(solution)/shard_map/gather | solution.py:30
  399.6 8.7 %copy.77 = bf16[4,512,1536]{1,2,0:T(8,128)(2,1)} copy(bf16[4,512,1536]{2,1,0:T(8,128)(2,1)} %gather_fusion) | data formatting | bytes 12582912 | tf_op jit(solution)/shard_map/gather | solution.py:30
  408.3 6.3 %gather_fusion.1 = bf16[4,512,1536]{2,1,0:T(8,128)(2,1)} fusion(bf16[4,512,1536]{2,1,0:T(8,128)(2,1)} %get-tuple-element.248, s32[1024]{0:T(1024)S(1)} %pad_clamp_fusion), kind=kCustom, calls=%fused_computation.1 | custom fusion | bytes 12582928 | tf_op jit(solution)/shard_map/gather | solution.py:30
  414.6 8.6 %copy.78 = bf16[4,512,1536]{1,2,0:T(8,128)(2,1)} copy(bf16[4,512,1536]{2,1,0:T(8,128)(2,1)} %gather_fusion.1) | data formatting | bytes 12582912 | tf_op jit(solution)/shard_map/gather | solution.py:30
  423.3 7.8 %convert_reduce_fusion.1 = f32[3072,128]{1,0:T(8,128)} fusion(bf16[128,4,512]{2,0,1:T(8,128)(2,1)S(1)} %bitcast.166, bf16[4,512,1536]{1,2,0:T(8,128)(2,1)} %copy.78, bf16[4,512,1536]{1,2,0:T(8,128)(2,1)} %copy.77), kind=kOutput, calls=%fused_computation.69 | convolution fusion | flops 1640103936 | bytes 14680064 | tf_op jit(solution)/shard_map/rgc,gcd->rgd/dot_general | solution.py:111
  435.0 41.5 %psum.7 = f32[]{:T(128)} all-reduce(f32[]{:T(128)} %fusion.76), channel_id=1, replica_groups=mesh['frame'=4,'space'=8] {'frame','space'}, use_global_device_ids=true, to_apply=%region_18.19 | all-reduce | flops 1 | bytes 8 | tf_op jit(solution)/shard_map/psum | solution.py:186
  (133 shorter events, 51.9 us)
Async XLA Ops:
  7.2 55.0 %all-gather.4.cloned.1.call-start = ((), (), s32[]{:S(2)}) async-start(), calls=%async_computation.2 | async-start | bytes 7077888 | tf_op jit(solution)/shard_map/all_gather | solution.py:128
  8.0 5.7 %copy-start = (bf16[2,1,64,3072]{3,2,1,0:T(8,128)(2,1)S(1)}, bf16[2,1,64,3072]{3,2,1,0:T(8,128)(2,1)}, u32[]{:S(2)}) copy-start(bf16[2,1,64,3072]{3,2,1,0:T(8,128)(2,1)} %param.16) | copy-start | bytes 2359300
  13.1 3.3 copy-start.5
  15.6 120.3 %all-gather.6.cloned.1.call-start = ((), (), s32[]{:S(2)}) async-start(), calls=%async_computation.3 | async-start | bytes 14155776 | tf_op jit(solution)/shard_map/all_gather | solution.py:145
  62.1 9.9 %copy-start.3 = (s32[2,16,16]{2,1,0:T(8,128)S(1)}, s32[2,16,16]{2,1,0:T(8,128)}, u32[]{:S(2)}) copy-start(s32[2,16,16]{2,1,0:T(8,128)} %param.20) | copy-start | bytes 6148
  86.1 12.5 %all-to-all-start = ((bf16[512,2,1,256]{3,1,2,0:T(2,128)(2,1)}), bf16[512,2,1,256]{3,1,2,0:T(2,128)(2,1)S(1)}, u32[]{:S(2)}, u32[]{:S(2)}) async-start(bf16[512,2,1,256]{3,1,2,0:T(2,128)(2,1)} %bitcast.119), calls=%async_computation | async-start | bytes 1048576 | tf_op jit(solution)/shard_map/all_to_all | solution.py:146
  90.3 265.4 %all-gather.8.cloned.1.call-start = ((), (), s32[]{:S(2)}) async-start(), calls=%async_computation.4 | async-start | bytes 3932160 | tf_op jit(solution)/shard_map/all_gather | solution.py:159
  90.3 75.6 %collective-permute-start = (bf16[512,3072]{1,0:T(8,128)(2,1)}, bf16[512,3072]{1,0:T(8,128)(2,1)}, u32[]{:S(2)}, u32[]{:S(2)}) collective-permute-start(bf16[512,3072]{1,0:T(8,128)(2,1)} %param.25), channel_id=1, source_target_pairs={{0,8},{8,16},{16,24},{24,0},{1,9},{9,17},{17,25},{25,1},{2,10},{10... | collective-permute-start | bytes 9437192 | tf_op jit(solution)/shard_map/ppermute | solution.py:25
  148.3 148.4 %collective-permute-start.2 = (bf16[512,3072]{1,0:T(8,128)(2,1)}, bf16[512,3072]{1,0:T(8,128)(2,1)}, u32[]{:S(2)}, u32[]{:S(2)}) collective-permute-start(bf16[512,3072]{1,0:T(8,128)(2,1)} %param.25), channel_id=1, source_target_pairs={{8,0},{16,8},{24,16},{0,24},{9,1},{17,9},{25,17},{1,25},{10,2},{18... | collective-permute-start | bytes 9437192 | tf_op jit(solution)/shard_map/ppermute | solution.py:27
  165.9 180.3 %collective-permute-start.1 = (bf16[512,3072]{1,0:T(8,128)(2,1)}, bf16[512,3072]{1,0:T(8,128)(2,1)}, u32[]{:S(2)}, u32[]{:S(2)}) collective-permute-start(bf16[512,3072]{1,0:T(8,128)(2,1)} %collective-permute-done), channel_id=1, source_target_pairs={{0,8},{8,16},{16,24},{24,0},{1,9},{9,17},{17,25},{25,1},{2,10},{10... | collective-permute-start | bytes 9437192 | tf_op jit(solution)/shard_map/ppermute | solution.py:25
  175.1 171.0 %copy-start.1 = (bf16[512,3072]{1,0:T(8,128)(2,1)S(1)}, bf16[512,3072]{1,0:T(8,128)(2,1)}, u32[]{:S(2)}) copy-start(bf16[512,3072]{1,0:T(8,128)(2,1)} %param.25) | copy-start | bytes 9437188
  377.1 46.1 %all-to-all-start.1 = ((bf16[4,2,64,512]{3,2,1,0:T(8,128)(2,1)}), bf16[4,2,64,512]{3,2,1,0:T(8,128)(2,1)S(1)}, u32[]{:S(2)}, u32[]{:S(2)}) async-start(bf16[4,2,64,512]{3,2,1,0:T(8,128)(2,1)} %bitcast.165), calls=%async_computation.1 | async-start | bytes 1048576 | tf_op jit(solution)/shard_map/all_to_all | solution.py:171
  431.0 2.0 copy-start.2
  431.0 2.0 copy-start.4
Sparse Core Ops, SparseCore 0:
  15.7 46.3 all-gather.3
  64.0 71.8 all-gather.5
  148.4 152.0 all-gather.7
